TPU v7x, 32 devices: a whole 2x2x4 slice. The times are simulated.
32 devices in a mesh: grp: 2 (over y), ep: 8 (over z, x), seq: 1, rep: 2 (over core).
Axes of the slice: x: 2, y: 2, z: 4, core: 2. Of those that a mesh axis runs over, the one named last changes fastest.
Arguments:
- hidden_in: bfloat16 [1024, 2048], P(('grp', 'ep', 'rep'), 'seq'), parts along dimension 0, may hold values from -64 to 64
- row_counts: int32 [32], P(('grp', 'ep', 'rep')), parts along dimension 0, may hold values from 24 to 32, as said below
- qkv_new: bfloat16 [1024, 3, 2048], P(('grp', 'ep', 'rep')), parts along dimension 0, may hold values from -6 to 6
- cache_len: int32 [16, 64], P('grp', ('rep', 'seq')), parts along dimension 0, may hold values from 1 to 128, as said below
- kv_cache: bfloat16 [2, 16, 64, 128, 2048], P(None, 'grp', ('rep', 'seq'), None, 'ep'), parts along dimension 1, may hold values from -128 to 128
- w_out: bfloat16 [2048, 2048], P('ep', 'seq'), may hold values from -0.125 to 0.125
- moe_gain: float32 [2048], replicated, may hold values from 0.1 to 1.9
- w_in: bfloat16 [16, 2048, 2, 1408], P(('ep', 'rep'), None, None, 'seq'), may hold values from -0.125 to 0.125
- w_down: bfloat16 [16, 1408, 2048], P(('ep', 'rep'), 'seq'), may hold values from -0.15625 to 0.15625
- route_ids: int32 [1024, 6], P(('grp', 'ep', 'rep')), parts along dimension 0, may hold values from 0 to 15, all different within a row; in each aligned block of 32 rows (0 to 31, 32 to 63, ...) at most 24 rows name the same one
- route_weight: bfloat16 [1024, 6], P(('grp', 'ep', 'rep')), parts along dimension 0, may hold values from 0.049804688 to 0.44921875
Outputs:
- mixed: bfloat16 [1024, 2048], P(('grp', 'ep', 'rep'), 'seq'), parts along dimension 0
There are 2 independent parts, one for each index of `grp`. A program takes and returns all parts, laid end to end along the dimension named above; an argument that names none is the same for every part. Nothing has to cross between parts.
Inputs may be any that keep to these rules, and one draw needn't show every extreme that they name: The first row_counts[b] slots of block b are live; some block is full. `cache_len`: some row has 128 cached positions. `route_ids`: a row's 6 experts differ; among the 32 rows of one block no expert is named by more than 24 rows, and in some block one is named by exactly 24.
All inputs are finite; a program needn't handle non-finite values.
Results may differ from a plain program's by a relative error of at most 0.0053.
Values may be sent and summed in bfloat16 or wider, within the bound.
A program may use at most 192 MiB of HBM per device.

v0:
```python
import math

import jax
import jax.numpy as jnp
from jax import lax
from jax.sharding import PartitionSpec as P

D = 2048
HEAD_DIM = 128
TOPK = 6


epsilon = 1e-06
masked_score = -1e30


def local(
    hidden_in,
    row_counts,
    qkv_new,
    cache_len,
    kv_cache,
    w_out,
    moe_gain,
    w_in,
    w_down,
    route_ids,
    route_weight,
):
    tok_rows, feat_local = hidden_in.shape
    owners = lax.axis_size("ep")
    parts_seq = lax.axis_size("seq")
    width_local = kv_cache.shape[-1]
    heads_local = width_local // HEAD_DIM
    positions = kv_cache.shape[3]
    share_rows = tok_rows // parts_seq
    attend_rows = owners * share_rows
    moved_block = lax.all_to_all(qkv_new, "ep", split_axis=2, concat_axis=0, tiled=True)
    moved_block = moved_block.reshape(owners, tok_rows, 3, width_local)
    heads_block = lax.dynamic_slice_in_dim(
        moved_block, lax.axis_index("seq") * share_rows, share_rows, 1
    )
    heads_block = heads_block.reshape(attend_rows, 3, heads_local, HEAD_DIM)
    queries = heads_block[:, 0]
    key_new = heads_block[:, 1].astype(jnp.float32)
    value_new = heads_block[:, 2].astype(jnp.float32)
    lengths = cache_len.reshape(attend_rows)
    cache_keys = kv_cache[0].reshape(attend_rows, positions, heads_local, HEAD_DIM)
    cache_values = kv_cache[1].reshape(attend_rows, positions, heads_local, HEAD_DIM)
    score_scale = 1.0 / math.sqrt(HEAD_DIM)
    position = jnp.arange(positions, dtype=jnp.int32)
    in_cache = position[None, None, :] < lengths[:, None, None]
    scores = (
        jnp.einsum("nhd,nphd->nhp", queries, cache_keys, preferred_element_type=jnp.float32)
        * score_scale
    )
    scores = jnp.where(in_cache, scores, masked_score)
    own_score = jnp.sum(queries.astype(jnp.float32) * key_new, axis=2) * score_scale
    highest = jnp.maximum(jnp.max(scores, axis=2), own_score)
    weights = jnp.where(in_cache, jnp.exp(scores - highest[..., None]), 0.0)
    partial_sum = jnp.einsum(
        "nhp,nphd->nhd",
        weights.astype(jnp.bfloat16),
        cache_values,
        preferred_element_type=jnp.float32,
    )
    own_weight = jnp.exp(own_score - highest)
    attended = (partial_sum + own_weight[..., None] * value_new) / (
        jnp.sum(weights, axis=2) + own_weight
    )[..., None]
    attended = attended.astype(jnp.bfloat16).reshape(owners, share_rows, width_local)
    attended = lax.all_gather(attended, "seq", axis=1, tiled=True).reshape(
        owners * tok_rows, width_local
    )
    attn_out = lax.psum_scatter(
        jnp.dot(attended, w_out, preferred_element_type=jnp.float32),
        "ep",
        scatter_dimension=0,
        tiled=True,
    )
    residual = (hidden_in.astype(jnp.float32) + attn_out).astype(jnp.bfloat16)
    residual_wide = lax.optimization_barrier(residual).astype(jnp.float32)
    is_live = jnp.arange(tok_rows, dtype=jnp.int32) < row_counts[0]
    expert_total = lax.axis_size(("ep", "rep")) * w_in.shape[0]
    capacity = min(tok_rows, max(2, 2 * tok_rows * TOPK // expert_total))
    pair_count = tok_rows * TOPK
    flat_ids = route_ids.reshape(pair_count)
    pair_hits = (
        flat_ids[:, None] == jnp.arange(expert_total, dtype=jnp.int32)[None, :]
    ) & jnp.repeat(is_live, TOPK)[:, None]
    hit_counts = pair_hits.astype(jnp.int32)
    earlier_hits = jnp.cumsum(hit_counts, axis=0) - hit_counts
    slot_index = jnp.sum(earlier_hits * hit_counts, axis=1)
    target_cell = jnp.where(
        jnp.any(pair_hits, axis=1), flat_ids * capacity + slot_index, -1
    ).reshape(tok_rows, TOPK)
    cell_index = jnp.arange(expert_total * capacity, dtype=jnp.int32)
    cell_hits = target_cell[None, :, :] == cell_index[:, None, None]
    dispatch_rows = jnp.any(cell_hits, axis=2).astype(jnp.bfloat16)
    combine_rows = jnp.sum(
        jnp.where(cell_hits, route_weight.astype(jnp.float32)[None], 0.0), axis=2
    ).astype(jnp.bfloat16)
    full_rows = lax.all_gather(residual, "seq", axis=1, tiled=True)
    rows_wide = full_rows.astype(jnp.float32)
    inverse_rms = lax.rsqrt(jnp.mean(rows_wide * rows_wide, axis=1) + epsilon)
    normed = (rows_wide * inverse_rms[:, None] * moe_gain).astype(jnp.bfloat16)
    outgoing = jnp.dot(dispatch_rows, normed, preferred_element_type=jnp.float32).astype(
        jnp.bfloat16
    )
    outgoing = outgoing.reshape(expert_total, capacity, D)
    arrived = lax.all_to_all(outgoing, ("ep", "rep"), split_axis=0, concat_axis=0, tiled=True)
    sources, slot_count, feature_count = arrived.shape
    flat_rows = arrived.reshape(sources * slot_count, D)
    gate_up = jnp.dot(flat_rows, w_in.reshape(D, -1), preferred_element_type=jnp.float32).reshape(
        sources * slot_count, 2, -1
    )
    hidden_units = (jax.nn.silu(gate_up[:, 0]) * gate_up[:, 1]).astype(jnp.bfloat16)
    down_part = jnp.dot(
        hidden_units, w_down.reshape(-1, D), preferred_element_type=jnp.float32
    ).reshape(sources, slot_count, D)
    summed = lax.psum_scatter(down_part, "seq", scatter_dimension=2, tiled=True).astype(
        jnp.bfloat16
    )
    returned = lax.all_to_all(summed, ("ep", "rep"), split_axis=0, concat_axis=0, tiled=True)
    returned = returned.reshape(expert_total * capacity, feat_local)
    moe_out = lax.dot_general(
        combine_rows, returned, (((0,), (0,)), ((), ())), preferred_element_type=jnp.float32
    )
    mixed = jnp.where(is_live[:, None], residual_wide + moe_out, 0.0).astype(jnp.bfloat16)
    return mixed


def solution(mesh):
    placed = (
        P(("grp", "ep", "rep"), "seq"),
        P(("grp", "ep", "rep")),
        P(("grp", "ep", "rep"), None, None),
        P("grp", ("rep", "seq")),
        P(None, "grp", ("rep", "seq"), None, "ep"),
        P("ep", "seq"),
        P(),
        P(("ep", "rep"), None, None, "seq"),
        P(("ep", "rep"), "seq", None),
        P(("grp", "ep", "rep"), None),
        P(("grp", "ep", "rep"), None),
    )
    return jax.shard_map(
        local, mesh=mesh, in_specs=placed, out_specs=P(("grp", "ep", "rep"), "seq"), check_vma=False
    )
```

profile of v0, /device:TPU:13, one launch (start us, length us, event | category | flops | bytes accessed | tf_op | source)
XLA Modules:
  0.0 287.0 jit_solution(12234026153400670893)
XLA Ops:
  6.5 0.0 copy-start
  6.5 2.9 copy.41
  9.4 2.5 reshape.133
  11.9 5.7 %all-to-all-start = ((bf16[8,2,12288]{2,1,0:T(2,128)(2,1)}), bf16[8,2,12288]{2,1,0:T(2,128)(2,1)S(1)}, u32[]{:S(2)}, u32[]{:S(2)}) async-start(bf16[8,2,12288]{2,1,0:T(2,128)(2,1)} %reshape.133), calls=%async_computation | async-start | bytes 786432 | tf_op jit(solution)/shard_map/all_to_all | solution.py:38
  17.6 0.0 reduce-scatter.2.cloned.1.call-start
  17.6 23.1 %fusion.39 = (bf16[1,8,32,128,256]{4,3,2,1,0:T(8,128)(2,1)}, bf16[1,8,32,128,256]{4,3,2,1,0:T(8,128)(2,1)}) fusion(bf16[2,8,32,128,256]{4,3,2,1,0:T(8,128)(2,1)} %param.15), kind=kLoop, calls=%fused_computation.65 | loop fusion | bytes 67108864 | tf_op jit(solution)/shard_map/slice | solution.py:48
  40.7 23.7 %reshape_squeeze.7 = bf16[256,128,2,128]{3,2,1,0:T(2,128)(2,1)} reshape(bf16[1,8,32,128,256]{4,3,2,1,0:T(8,128)(2,1)} %get-tuple-element.10) | data formatting | bytes 33554432 | tf_op jit(solution)/shard_map/reshape;squeeze | solution.py:49
  64.4 0.0 copy-start.5
  64.4 21.2 %copy.58 = bf16[1,8,32,128,256]{3,4,2,1,0:T(8,128)(2,1)} copy(bf16[1,8,32,128,256]{4,3,2,1,0:T(8,128)(2,1)} %get-tuple-element.9) | data formatting | bytes 33554432 | tf_op jit(solution)/shard_map/reshape;squeeze | solution.py:48
  85.6 0.0 copy-done.5
  85.6 0.1 lt.34
  85.7 0.7 iota_compare_fusion.1
  86.4 0.0 all-to-all-done
  86.4 1.3 reshape.134
  87.8 1.0 copy.42
  88.8 0.1 reshape.114
  88.9 0.1 slice_bitcast_fusion.2
  89.0 0.3 fusion.16
  89.4 0.1 copy.43
  89.4 0.0 copy-start.1
  89.4 8.1 %fusion.19 = f32[256,2,1,128]{3,2,1,0:T(1,128)S(1)} fusion(bf16[256,128,2,128]{1,3,2,0:T(8,128)(2,1)} %bitcast.85, bf16[256,2,128,1]{2,1,0,3:T(2,128)(2,1)S(1)} %slice_bitcast_fusion.2), kind=kOutput, calls=%fused_computation.27 | convolution fusion | flops 16777216 | bytes 17170432 | tf_op jit(solution)/shard_map/nhd,nphd->nhp/dot_general | solution.py:54
  97.5 0.0 copy-done.1
  97.5 0.2 fusion.24
  97.7 0.3 fusion.22
  97.9 0.1 copy.45
  98.1 0.1 copy.44
  98.2 9.0 %fusion = f32[256,2,1,128]{3,2,1,0:T(1,128)S(1)} fusion(bf16[256,128,2,128]{3,2,1,0:T(2,128)(2,1)} %reshape_squeeze.7, bf16[256,2,128,1]{2,0,1,3:T(8,128)(2,1)S(1)} %get-tuple-element.12), kind=kOutput, calls=%fused_computation | convolution fusion | flops 16777216 | bytes 17170432 | tf_op jit(solution)/shard_map/nhp,nphd->nhd/dot_general | solution.py:61
  107.2 0.0 copy-start.4
  107.2 0.0 copy-start.2
  107.2 0.7 fusion.21
  107.9 0.0 copy-start.3
  107.9 0.0 copy-done
  107.9 1.8 fusion.27
  109.7 0.0 reduce-scatter.2.cloned.1.call-update
  109.8 0.0 copy-done.4
  109.8 0.1 copy.46
  109.9 0.1 eq.35
  110.6 0.1 broadcast_in_dim.63
  110.7 0.1 and.16
  110.9 0.1 reduce_or.21
  111.0 0.6 reduce-window.6
  111.6 0.2 slice_reduce_fusion
  111.8 0.1 bitcast_bitcast_fusion
  111.9 0.1 reduce_sum.50
  112.1 0.1 copy.50
  112.1 0.1 fusion.10
  112.3 66.0 %reduce-scatter.2.cloned.1.call-done = f32[32,2048]{1,0:T(8,128)} async-done(((f32[256,2048]{1,0:T(8,128)}), f32[32,2048]{1,0:T(8,128)}) %reduce-scatter.2.cloned.1.call-update) | async-done | bytes 262160 | tf_op jit(solution)/shard_map/reduce_scatter | solution.py:75
  178.2 0.0 copy-done.2
  178.2 1.1 fusion.11
  179.3 0.0 copy-done.3
  179.3 1.8 convolution_convert_fusion
  181.1 6.4 %all-to-all-start.1 = ((bf16[16,24,2048]{2,1,0:T(8,128)(2,1)}), bf16[16,24,2048]{2,1,0:T(8,128)(2,1)S(1)}, u32[]{:S(2)}, u32[]{:S(2)}) async-start(bf16[16,24,2048]{2,1,0:T(8,128)(2,1)} %bitcast.13), calls=%async_computation.2 | async-start | bytes 3145728 | tf_op jit(solution)/shard_map/all_to_all | solution.py:111
  187.5 11.3 %copy.62 = bf16[256,8,2,1408]{3,1,2,0:T(8,128)(2,1)} copy(bf16[256,8,2,1408]{3,2,1,0:T(2,128)(2,1)} %bitcast.87) | data formatting | bytes 23068672
  198.8 15.1 %copy.51 = bf16[2816,2048]{1,0:T(8,128)(2,1)} copy(bf16[2816,2048]{0,1:T(8,128)(2,1)} %bitcast.86) | data formatting | bytes 23068672 | tf_op jit(solution)/shard_map/dot_general | solution.py:114
  213.9 9.1 %all-to-all-done.1 = bf16[16,24,2048]{2,1,0:T(8,128)(2,1)S(1)} async-done(((bf16[16,24,2048]{2,1,0:T(8,128)(2,1)}), bf16[16,24,2048]{2,1,0:T(8,128)(2,1)S(1)}, u32[]{:S(2)}, u32[]{:S(2)}) %all-to-all-start.1) | async-done | bytes 1572896 | tf_op jit(solution)/shard_map/all_to_all | solution.py:111
  223.1 7.9 %fusion.40 = f32[384,2,1408]{2,0,1:T(8,128)S(1)} fusion(bf16[384,2048,1]{1,0,2:T(8,128)(2,1)S(1)} %bitcast.92, bf16[2,1408,2048]{2,1,0:T(8,128)(2,1)} %bitcast.88), kind=kOutput, calls=%fused_computation.66 | convolution fusion | flops 4429185024 | bytes 17432576 | tf_op jit(solution)/shard_map/dot_general | solution.py:114
  231.0 0.6 fusion.9
  231.7 6.4 %fusion.4 = bf16[16,24,2048]{2,1,0:T(8,128)(2,1)} fusion(bf16[16,24,1408]{2,1,0:T(8,128)(2,1)S(1)} %bitcast.94, bf16[1,1408,2048]{2,1,0:T(8,128)(2,1)} %param.19), kind=kOutput, calls=%fused_computation.4 | convolution fusion | flops 2215378944 | bytes 8421376 | tf_op jit(solution)/shard_map/dot_general | solution.py:118
  238.0 0.0 copy-start.6
  238.0 5.6 %all-to-all-start.2 = ((bf16[16,24,2048]{2,1,0:T(8,128)(2,1)}), bf16[16,24,2048]{2,1,0:T(8,128)(2,1)S(1)}, u32[]{:S(2)}, u32[]{:S(2)}) async-start(bf16[16,24,2048]{2,1,0:T(8,128)(2,1)} %fusion.4), calls=%async_computation.3 | async-start | bytes 3145728 | tf_op jit(solution)/shard_map/all_to_all | solution.py:124
  243.6 0.0 copy-done.6
  243.6 0.1 select_reduce_fusion
  243.7 35.4 %all-to-all-done.2 = bf16[16,24,2048]{2,1,0:T(8,128)(2,1)S(1)} async-done(((bf16[16,24,2048]{2,1,0:T(8,128)(2,1)}), bf16[16,24,2048]{2,1,0:T(8,128)(2,1)S(1)}, u32[]{:S(2)}, u32[]{:S(2)}) %all-to-all-start.2) | async-done | bytes 1572896 | tf_op jit(solution)/shard_map/all_to_all | solution.py:124
  279.1 1.0 fusion.8
  (12 shorter events, 0.2 us)
Async XLA Ops:
  6.5 101.4 %copy-start = (bf16[256,2048]{1,0:T(8,128)(2,1)S(1)}, bf16[256,2048]{1,0:T(8,128)(2,1)}, u32[]{:S(2)}) copy-start(bf16[256,2048]{1,0:T(8,128)(2,1)} %param.16) | copy-start | bytes 3145732
  11.9 74.6 %all-to-all-start = ((bf16[8,2,12288]{2,1,0:T(2,128)(2,1)}), bf16[8,2,12288]{2,1,0:T(2,128)(2,1)S(1)}, u32[]{:S(2)}, u32[]{:S(2)}) async-start(bf16[8,2,12288]{2,1,0:T(2,128)(2,1)} %reshape.133), calls=%async_computation | async-start | bytes 786432 | tf_op jit(solution)/shard_map/all_to_all | solution.py:38
  17.6 160.7 %reduce-scatter.2.cloned.1.call-start = ((), (), s32[]{:S(2)}) async-start(), calls=%async_computation.4 | async-start | bytes 2359296 | tf_op jit(solution)/shard_map/reduce_scatter | solution.py:75
  64.4 21.2 %copy-start.5 = (s32[8,32]{1,0:T(8,128)S(1)}, s32[8,32]{1,0:T(8,128)}, u32[]{:S(2)}) copy-start(s32[8,32]{1,0:T(8,128)} %param.14) | copy-start | bytes 3076
  89.4 8.1 %copy-start.1 = (pred[256,128]{1,0:T(8,128)(4,1)S(1)}, pred[256,128]{1,0:T(8,128)(4,1)}, u32[]{:S(2)}) copy-start(pred[256,128]{1,0:T(8,128)(4,1)} %iota_compare_fusion.1) | copy-start | bytes 98308
  107.2 2.6 copy-start.4
  107.2 71.0 %copy-start.2 = (bf16[32,2048]{1,0:T(8,128)(2,1)S(1)}, bf16[32,2048]{1,0:T(8,128)(2,1)}, u32[]{:S(2)}) copy-start(bf16[32,2048]{1,0:T(8,128)(2,1)} %param.11) | copy-start | bytes 393220
  107.9 71.4 %copy-start.3 = (f32[2048]{0:T(1024)S(1)}, f32[2048]{0:T(1024)}, u32[]{:S(2)}) copy-start(f32[2048]{0:T(1024)} %param.17) | copy-start | bytes 24580
  181.1 42.0 %all-to-all-start.1 = ((bf16[16,24,2048]{2,1,0:T(8,128)(2,1)}), bf16[16,24,2048]{2,1,0:T(8,128)(2,1)S(1)}, u32[]{:S(2)}, u32[]{:S(2)}) async-start(bf16[16,24,2048]{2,1,0:T(8,128)(2,1)} %bitcast.13), calls=%async_computation.2 | async-start | bytes 3145728 | tf_op jit(solution)/shard_map/all_to_all | solution.py:111
  238.0 5.6 %copy-start.6 = (bf16[32,6]{0,1:T(8,128)(2,1)S(1)}, bf16[32,6]{0,1:T(8,128)(2,1)}, u32[]{:S(2)}) copy-start(bf16[32,6]{0,1:T(8,128)(2,1)} %param.21) | copy-start | bytes 1156
  238.0 41.1 %all-to-all-start.2 = ((bf16[16,24,2048]{2,1,0:T(8,128)(2,1)}), bf16[16,24,2048]{2,1,0:T(8,128)(2,1)S(1)}, u32[]{:S(2)}, u32[]{:S(2)}) async-start(bf16[16,24,2048]{2,1,0:T(8,128)(2,1)} %fusion.4), calls=%async_computation.3 | async-start | bytes 3145728 | tf_op jit(solution)/shard_map/all_to_all | solution.py:124
Sparse Core Ops, SparseCore 0:
  109.9 68.2 reduce-scatter.1
where the time goes:
time: 290 us; the launch traced here: 287 us
  waiting for transfers between devices  111 us (38%)
  local copies, waits for them, and re-layouts  104 us (36%)
  matrix products  35.9 us (12%)
  starting transfers between devices  17.7 us (6%)
  between operations  14.3 us (5%)
  other arithmetic  4.97 us (2%)
    reduce_scatter x1, waiting for transfers between devices, local(): lax.psum_scatter(jnp.dot(attended, w_out, preferred_element_type=jnp.floa...  66 us
    all_to_all x1, waiting for transfers between devices, local(): lax.all_to_all(summed, ('ep', 'rep'), split_axis=0, concat_axis=0, tiled=...  35.4 us
    another operation x1, local copies, waits for them, and re-layouts, local(): kv_cache[1].reshape(attend_rows, positions, heads_local, HEAD_DIM)  23.7 us
    slice x1, local copies, waits for them, and re-layouts, local(): kv_cache[0].reshape(attend_rows, positions, heads_local, HEAD_DIM)  23.1 us
    another operation x1, local copies, waits for them, and re-layouts, local(): kv_cache[0].reshape(attend_rows, positions, heads_local, HEAD_DIM)  21.2 us
    unnamed x19, local copies, waits for them, and re-layouts  18 us
    dot_general x1, local copies, waits for them, and re-layouts, local(): jnp.dot(flat_rows, w_in.reshape(D, -1), preferred_element_type=jnp.float32)  15.1 us
    all_to_all x1, waiting for transfers between devices, local(): lax.all_to_all(outgoing, ('ep', 'rep'), split_axis=0, concat_axis=0, tile...  9.15 us
  transfers between devices with their start and end apart: 4, of which 3 were waited for; matrix products, arithmetic and copies ran while one was open for 34% of the time, Pallas kernels for 0%

commit v1 on v0

--- a/solution.py
+++ b/solution.py
@@ -1,8 +1,11 @@
+import functools
 import math
 
 import jax
 import jax.numpy as jnp
 from jax import lax
+from jax.experimental import pallas as pl
+from jax.experimental.pallas import tpu as pltpu
 from jax.sharding import PartitionSpec as P
 
 D = 2048
@@ -130,6 +133,459 @@
     return mixed
 
 
+LANES = 128
+F32 = jnp.float32
+BF16 = jnp.bfloat16
+
+
+def layer_kernel(
+    owners,
+    qkv_ref,
+    lens_ref,
+    kv_hbm,
+    w_out_ref,
+    hidden_ref,
+    gain_ref,
+    coef_ref,
+    live_ref,
+    w_in_hbm,
+    w_down_hbm,
+    out_ref,
+    kv_buf,
+    q_buf,
+    pair_out,
+    pair_in,
+    col_out,
+    col_in,
+    total,
+    rows_all,
+    w_in_buf,
+    w_down_buf,
+    hidden_buf,
+    y_out,
+    y_in,
+    y_own,
+    pair_out2,
+    pair_in2,
+    col_out2,
+    col_in2,
+    kv_sem,
+    w_sem,
+    q_send,
+    q_recv,
+    pair_send,
+    pair_recv,
+    col_send,
+    col_recv,
+    z_send,
+    x_send,
+    s_send,
+    g_recv,
+    y_send,
+    y_recv,
+    pair_send2,
+    pair_recv2,
+    col_send2,
+    col_recv2,
+):
+    cols = owners // 2
+    me = lax.axis_index("ep")
+    rep = lax.axis_index("rep")
+    mz, mx = me // 2, me % 2
+    across = mz * 2 + (1 - mx)
+    sister = 1 - rep
+    block, width = hidden_ref.shape
+    part = kv_buf.shape[-1]
+    positions = kv_buf.shape[-2]
+    heads = part // HEAD_DIM
+    used = heads * block
+
+    def remote(src, dst, send, recv, ep=None, core=None):
+        return pltpu.make_async_remote_copy(
+            src_ref=src,
+            dst_ref=dst,
+            send_sem=send,
+            recv_sem=recv,
+            device_id={"ep": me if ep is None else ep, "rep": rep if core is None else core},
+            device_id_type=pl.DeviceIdType.MESH,
+        )
+
+    def kv_copy(owner, slot):
+        return pltpu.make_async_copy(kv_hbm.at[:, owner], kv_buf.at[slot], kv_sem.at[slot])
+
+    def owner_of(j, s):
+        z = (mz + 1 + j) % cols
+        return z * 2 + (1 - mx if s == 0 else mx)
+
+    in_copy = pltpu.make_async_copy(w_in_hbm, w_in_buf, w_sem.at[0])
+    down_copy = pltpu.make_async_copy(w_down_hbm, w_down_buf, w_sem.at[1])
+    kv_copy(owner_of(0, 0), 0).start()
+    kv_copy(owner_of(0, 1), 1).start()
+    in_copy.start()
+    down_copy.start()
+
+    barrier = pltpu.get_barrier_semaphore()
+    for i in range(1, owners):
+        pl.semaphore_signal(
+            barrier,
+            inc=1,
+            device_id={"ep": (me + i) % owners, "rep": rep},
+            device_id_type=pl.DeviceIdType.MESH,
+        )
+    pl.semaphore_signal(
+        barrier, inc=1, device_id={"ep": me, "rep": sister}, device_id_type=pl.DeviceIdType.MESH
+    )
+    pl.semaphore_wait(barrier, owners)
+
+    def q_part(owner):
+        return qkv_ref.at[:, :, pl.ds(pl.multiple_of(owner * part, part), part)]
+
+    @pl.loop(1, owners)
+    def _(i):
+        to = (me + owners - i) % owners
+        remote(q_part(to), q_buf.at[me], q_send.at[to], q_recv.at[me], ep=to).start()
+
+    q_buf[me] = qkv_ref[:, :, pl.ds(pl.multiple_of(me * part, part), part)]
+
+    lane_row = lax.broadcasted_iota(jnp.int32, (positions, LANES), 1) % block
+    pos_of = lax.broadcasted_iota(jnp.int32, (positions, LANES), 0)
+    head_of = lax.broadcasted_iota(jnp.int32, (block, part), 1) // HEAD_DIM
+    row_mod = lax.broadcasted_iota(jnp.int32, (used, positions), 0) % block
+    scale = 1.0 / math.sqrt(HEAD_DIM)
+    group = 8
+
+    def partial(owner, slot):
+        query = q_buf[owner, 0]
+        fresh_k = q_buf[owner, 1]
+        fresh_v = q_buf[owner, 2].astype(F32)
+        zero = jnp.zeros_like(query)
+        stack = [jnp.where(head_of == h, query, zero) for h in range(heads)]
+        stack += [zero] * (LANES // block - heads)
+        queries = jnp.concatenate(stack, axis=0)
+        nt = (((1,), (1,)), ((), ()))
+
+        def score_step(g, acc):
+            keys = kv_buf[slot, 0, pl.ds(g * group, group)].reshape(group * positions, part)
+            got = lax.dot_general(keys, queries, nt, preferred_element_type=F32)
+            for r in range(group):
+                acc = jnp.where(
+                    lane_row == g * group + r, got[r * positions : (r + 1) * positions], acc
+                )
+            return acc
+
+        scores = lax.fori_loop(
+            0, block // group, score_step, jnp.zeros((positions, LANES), F32)
+        )
+        fresh = lax.dot_general(fresh_k, queries, nt, preferred_element_type=F32)
+        diag = lax.broadcasted_iota(jnp.int32, (block, LANES), 0) == (
+            lax.broadcasted_iota(jnp.int32, (block, LANES), 1) % block
+        )
+        own = jnp.sum(jnp.where(diag, fresh, 0.0), axis=0, keepdims=True) * scale
+        in_cache = pos_of < lens_ref[owner]
+        scores = jnp.where(in_cache, scores * scale, masked_score)
+        top = jnp.maximum(jnp.max(scores, axis=0, keepdims=True), own)
+        weights = jnp.where(in_cache, jnp.exp(scores - top), 0.0)
+        own_w = jnp.exp(own - top)
+        den = jnp.sum(weights, axis=0, keepdims=True) + own_w
+        own_t = jnp.broadcast_to(own_w, (LANES, LANES)).T
+        den_t = jnp.broadcast_to(den, (LANES, LANES)).T
+        weights_t = weights.T[:used]
+
+        def value_step(g, acc):
+            wide = jnp.concatenate(
+                [
+                    jnp.where(row_mod == g * group + r, weights_t, 0.0).astype(BF16)
+                    for r in range(group)
+                ],
+                axis=1,
+            )
+            values = kv_buf[slot, 1, pl.ds(g * group, group)].reshape(group * positions, part)
+            return acc + jnp.dot(wide, values, preferred_element_type=F32)
+
+        summed = lax.fori_loop(0, block // group, value_step, jnp.zeros((used, part), F32))
+        pieces = []
+        for h in range(heads):
+            rows = slice(h * block, (h + 1) * block)
+            lanes = slice(h * HEAD_DIM, (h + 1) * HEAD_DIM)
+            pieces.append((summed[rows, lanes] + own_t[rows] * fresh_v[:, lanes]) / den_t[rows])
+        attended = jnp.concatenate(pieces, axis=1).astype(BF16)
+        return jnp.dot(attended, w_out_ref[...], preferred_element_type=F32)
+
+    def arrive_q(owner):
+        @pl.when(owner != me)
+        def _():
+            remote(q_part(owner), q_buf.at[owner], q_send.at[owner], q_recv.at[owner], ep=owner).wait_recv()
+
+    def pair_copy(z):
+        return remote(pair_out.at[z], pair_in.at[z], pair_send.at[z], pair_recv.at[z], ep=across)
+
+    def col_copy(z, slot):
+        return remote(
+            col_out.at[z], col_in.at[slot], col_send.at[z], col_recv.at[slot], ep=z * 2 + mx
+        )
+
+    @pl.loop(0, cols)
+    def _(j):
+        z = (mz + 1 + j) % cols
+        first, second = owner_of(j, 0), owner_of(j, 1)
+        arrive_q(first)
+        kv_copy(first, 0).wait()
+        pair_out[z] = partial(first, 0).astype(BF16)
+        pair_copy(z).start()
+
+        @pl.when(j < cols - 1)
+        def _():
+            kv_copy(owner_of(j + 1, 0), 0).start()
+
+        arrive_q(second)
+        kv_copy(second, 1).wait()
+        mine = partial(second, 1)
+
+        @pl.when(j < cols - 1)
+        def _():
+            kv_copy(owner_of(j + 1, 1), 1).start()
+
+        pair_copy(z).wait_recv()
+        mine = mine + pair_in[z].astype(F32)
+
+        @pl.when(j < cols - 1)
+        def _():
+            col_out[z] = mine.astype(BF16)
+            col_copy(z, mz).start()
+
+        @pl.when(j == cols - 1)
+        def _():
+            total[...] = mine
+
+    for j in range(1, cols):
+        z = (mz + j) % cols
+        col_copy(z, z).wait_recv()
+        total[...] += col_in[z].astype(F32)
+    residual = (hidden_ref[...].astype(F32) + total[...]).astype(BF16)
+    wide = residual.astype(F32)
+    total[...] = wide
+    inverse = lax.rsqrt(jnp.mean(wide * wide, axis=1, keepdims=True) + epsilon)
+    rows_all[rep, me, :, :width] = (wide * inverse * gain_ref[...]).astype(BF16)
+    rows_all[rep, me, :, width:] = coef_ref[...]
+
+    def z_copy(z, e):
+        return remote(
+            rows_all.at[rep, e], rows_all.at[rep, e], z_send.at[z], g_recv.at[rep, e], ep=z * 2 + mx
+        )
+
+    def x_copy(e):
+        return remote(
+            rows_all.at[rep, e], rows_all.at[rep, e], x_send.at[e], g_recv.at[rep, e], ep=across
+        )
+
+    def s_copy(e, side):
+        return remote(
+            rows_all.at[side, e], rows_all.at[side, e], s_send.at[e], g_recv.at[side, e], core=sister
+        )
+
+    for j in range(1, cols):
+        z_copy((mz + j) % cols, me).start()
+    x_copy(me).start()
+    s_copy(me, rep).start()
+    for j in range(1, cols):
+        e = ((mz + j) % cols) * 2 + mx
+        z_copy(e // 2, e).wait_recv()
+        x_copy(e).start()
+        s_copy(e, rep).start()
+    for j in range(cols):
+        e = ((mz + j) % cols) * 2 + 1 - mx
+        x_copy(e).wait_recv()
+        s_copy(e, rep).start()
+    in_copy.wait()
+    down_copy.wait()
+
+    @pl.loop(0, owners)
+    def _(e):
+        s_copy(e, sister).wait_recv()
+
+    expert = me * 2 + rep
+    tiles = w_in_buf.shape[0]
+    half = owners * block
+    step = 2 * LANES
+
+    def experts(side, store):
+        @pl.loop(0, tiles)
+        def _(n):
+            rows = rows_all[side, :, :, :width].reshape(half, width)
+            both = jnp.dot(rows, w_in_buf[n], preferred_element_type=F32)
+            gate, up = both[:, :LANES], both[:, LANES:]
+            hidden_buf[:, pl.ds(pl.multiple_of(n * LANES, LANES), LANES)] = (
+                gate / (1.0 + jnp.exp(-gate)) * up
+            ).astype(BF16)
+
+        coefs = rows_all[side, :, :, width:].reshape(half, LANES).astype(F32)
+        lane = lax.broadcasted_iota(jnp.int32, (half, LANES), 1)
+        factor = jnp.sum(jnp.where(lane == expert, coefs, 0.0), axis=1, keepdims=True)
+
+        @pl.loop(0, width // step)
+        def _(n):
+            lanes = pl.ds(pl.multiple_of(n * step, step), step)
+            made = jnp.dot(hidden_buf[...], w_down_buf[:, lanes], preferred_element_type=F32)
+            store(lanes, (made.astype(BF16).astype(F32) * factor).reshape(owners, block, step))
+
+    def store_out(lanes, v):
+        y_out[:, :, lanes] = v.astype(BF16)
+
+    def store_own(lanes, v):
+        y_own[:, :, lanes] = v
+
+    experts(sister, store_out)
+    y_copy = remote(y_out, y_in, y_send, y_recv, core=sister)
+    y_copy.start()
+    experts(rep, store_own)
+    y_copy.wait()
+
+    def pair_copy2(z):
+        return remote(
+            pair_out2.at[z], pair_in2.at[z], pair_send2.at[z], pair_recv2.at[z], ep=across
+        )
+
+    def col_copy2(z, slot):
+        return remote(
+            col_out2.at[z], col_in2.at[slot], col_send2.at[z], col_recv2.at[slot], ep=z * 2 + mx
+        )
+
+    for j in range(cols):
+        z = (mz + 1 + j) % cols
+        e = z * 2 + 1 - mx
+        pair_out2[z] = (y_own[e] + y_in[e].astype(F32)).astype(BF16)
+        pair_copy2(z).start()
+    for j in range(cols):
+        z = (mz + 1 + j) % cols
+        e = z * 2 + mx
+        pair_copy2(z).wait_recv()
+        mine = y_own[e] + y_in[e].astype(F32) + pair_in2[z].astype(F32)
+        if j < cols - 1:
+            col_out2[z] = mine.astype(BF16)
+            col_copy2(z, mz).start()
+        else:
+            total[...] += mine
+    for j in range(1, cols):
+        z = (mz + j) % cols
+        col_copy2(z, z).wait_recv()
+        total[...] += col_in2[z].astype(F32)
+    out_ref[...] = jnp.where(live_ref[:, :1] > 0.0, total[...], 0.0).astype(BF16)
+
+    @pl.loop(1, owners)
+    def _(i):
+        to = (me + i) % owners
+        remote(q_part(to), q_buf.at[me], q_send.at[to], q_recv.at[me], ep=to).wait_send()
+
+    for z in range(cols):
+        pair_copy(z).wait_send()
+        pair_copy2(z).wait_send()
+    for j in range(1, cols):
+        z = (mz + j) % cols
+        col_copy(z, mz).wait_send()
+        col_copy2(z, mz).wait_send()
+        z_copy(z, me).wait_send()
+    for j in range(cols):
+        x_copy(((mz + j) % cols) * 2 + mx).wait_send()
+
+    @pl.loop(0, owners)
+    def _(e):
+        s_copy(e, rep).wait_send()
+
+
+def fast_local(
+    owners,
+    hidden_in,
+    row_counts,
+    qkv_new,
+    cache_len,
+    kv_cache,
+    w_out,
+    moe_gain,
+    w_in,
+    w_down,
+    route_ids,
+    route_weight,
+):
+    block, width = hidden_in.shape
+    part = kv_cache.shape[-1]
+    positions = kv_cache.shape[3]
+    cols = owners // 2
+    inner = w_down.shape[1]
+    tiles = inner // LANES
+    fresh = jnp.transpose(qkv_new, (1, 0, 2))
+    lens = jnp.tile(cache_len, (1, LANES // block)).reshape(owners, 1, LANES)
+    live = jnp.arange(block, dtype=jnp.int32) < row_counts[0]
+    lane = jnp.arange(LANES, dtype=jnp.int32)
+    hits = (route_ids[:, :, None] == lane[None, None, :]) & live[:, None, None]
+    coef = jnp.sum(jnp.where(hits, route_weight.astype(F32)[:, :, None], 0.0), axis=1).astype(BF16)
+    live_wide = jnp.broadcast_to(live[:, None], (block, LANES)).astype(F32)
+    w_tiles = jnp.transpose(w_in.reshape(width, 2, tiles, LANES), (2, 0, 1, 3)).reshape(
+        tiles, width, 2 * LANES
+    )
+    vmem = pl.BlockSpec(memory_space=pltpu.VMEM)
+    hbm = pl.BlockSpec(memory_space=pl.ANY)
+    dma = pltpu.SemaphoreType.DMA
+    wide = (cols, block, width)
+    return pl.pallas_call(
+        functools.partial(layer_kernel, owners),
+        out_shape=jax.ShapeDtypeStruct((block, width), BF16),
+        in_specs=[vmem, vmem, hbm, vmem, vmem, vmem, vmem, vmem, hbm, hbm],
+        out_specs=vmem,
+        scratch_shapes=[
+            pltpu.VMEM((2, 2, block, positions, part), BF16),
+            pltpu.VMEM((owners, 3, block, part), BF16),
+            pltpu.VMEM(wide, BF16),
+            pltpu.VMEM(wide, BF16),
+            pltpu.VMEM(wide, BF16),
+            pltpu.VMEM(wide, BF16),
+            pltpu.VMEM((block, width), F32),
+            pltpu.VMEM((2, owners, block, width + LANES), BF16),
+            pltpu.VMEM((tiles, width, 2 * LANES), BF16),
+            pltpu.VMEM((inner, width), BF16),
+            pltpu.VMEM((owners * block, inner), BF16),
+            pltpu.VMEM((owners, block, width), BF16),
+            pltpu.VMEM((owners, block, width), BF16),
+            pltpu.VMEM((owners, block, width), F32),
+            pltpu.VMEM(wide, BF16),
+            pltpu.VMEM(wide, BF16),
+            pltpu.VMEM(wide, BF16),
+            pltpu.VMEM(wide, BF16),
+            dma((2,)),
+            dma((2,)),
+            dma((owners,)),
+            dma((owners,)),
+            dma((cols,)),
+            dma((cols,)),
+            dma((cols,)),
+            dma((cols,)),
+            dma((cols,)),
+            dma((owners,)),
+            dma((owners,)),
+            dma((2, owners)),
+            dma(()),
+            dma(()),
+            dma((cols,)),
+            dma((cols,)),
+            dma((cols,)),
+            dma((cols,)),
+        ],
+        compiler_params=pltpu.CompilerParams(
+            collective_id=0, has_side_effects=True, vmem_limit_bytes=60 * 1024 * 1024
+        ),
+    )(
+        fresh,
+        lens,
+        kv_cache,
+        w_out,
+        hidden_in,
+        moe_gain.reshape(1, width),
+        coef,
+        live_wide,
+        w_tiles,
+        w_down.reshape(inner, width),
+    )
+
+
 def solution(mesh):
     placed = (
         P(("grp", "ep", "rep"), "seq"),
@@ -144,6 +600,10 @@
         P(("grp", "ep", "rep"), None),
         P(("grp", "ep", "rep"), None),
     )
+    sizes = mesh.shape
+    owners = sizes["ep"]
+    one_step = sizes["seq"] == 1 and sizes["rep"] == 2 and owners % 2 == 0 and owners <= 8
+    body = functools.partial(fast_local, owners) if one_step else local
     return jax.shard_map(
-        local, mesh=mesh, in_specs=placed, out_specs=P(("grp", "ep", "rep"), "seq"), check_vma=False
-    )
+        body, mesh=mesh, in_specs=placed, out_specs=P(("grp", "ep", "rep"), "seq"), check_vma=False
+    )

time: 290 us -> 181 us (0.62)
  waiting for transfers between devices: 111 us -> 0 us
  Pallas kernels: 0 us -> 97 us
  matrix products: 35.9 us -> 0 us
  local copies, waits for them, and re-layouts: 104 us -> 79.1 us
  starting transfers between devices: 17.7 us -> 0 us
  between operations: 14.3 us -> 0.67 us
    pallas_call x0 -> x1, Pallas kernels: none -> 97 us  [fast_local(): pl.pallas_call(functools.partial(layer_kernel, owners), out_shape=jax.Sha...]
    reduce_scatter x1 -> x0, waiting for transfers between devices: 66 us -> none  [local(): lax.psum_scatter(jnp.dot(attended, w_out, preferred_element_type=jnp.floa...]
    all_to_all x3 -> x0, waiting for transfers between devices: 44.6 us -> none  [the longest x1 35.4 us: local(): lax.all_to_all(summed, ('ep', 'rep'), split_axis=0, concat_axis=0, tiled=...]
    another operation x3 -> x2, local copies, waits for them, and re-layouts: 44.9 us -> 0.69 us  [fast_local(): lens = jnp.tile(cache_len, (1, LANES // block)).reshape(owners, 1, LANES)]
    dot_general x7 -> x0, matrix products: 35.9 us -> none  [the longest x1 8.97 us: local(): jnp.einsum('nhp,nphd->nhd', weights.astype(jnp.bfloat16), cache_values, p...]
    transpose x0 -> x1, local copies, waits for them, and re-layouts: none -> 28.6 us  [fast_local(): jnp.transpose(w_in.reshape(width, 2, tiles, LANES), (2, 0, 1, 3))]
    slice x2 -> x0, local copies, waits for them, and re-layouts: 23.3 us -> none  [the longest x1 23.1 us: local(): kv_cache[0].reshape(attend_rows, positions, heads_local, HEAD_DIM)]
    reshape x1, local copies, waits for them, and re-layouts: 0.1 us -> 18.9 us  [fast_local(): jnp.transpose(w_in.reshape(width, 2, tiles, LANES), (2, 0, 1, 3))]
  transfers between devices with their start and end apart: 4 -> 0, of which waited for: 3 -> 0; matrix products, arithmetic and copies ran while one was open for 34% -> 0% of each run, Pallas kernels for 0% -> 0%
where the time goes in v1:
time: 181 us; the launch traced here: 179 us
  Pallas kernels  97 us (54%)
  local copies, waits for them, and re-layouts  79.1 us (44%)
  other arithmetic  2.1 us (1%)
    pallas_call x1, Pallas kernels, fast_local(): pl.pallas_call(functools.partial(layer_kernel, owners), out_shape=jax.Sha...  97 us
    unnamed x4, local copies, waits for them, and re-layouts  30.2 us
    transpose x1, local copies, waits for them, and re-layouts, fast_local(): jnp.transpose(w_in.reshape(width, 2, tiles, LANES), (2, 0, 1, 3))  28.6 us
    reshape x1, local copies, waits for them, and re-layouts, fast_local(): jnp.transpose(w_in.reshape(width, 2, tiles, LANES), (2, 0, 1, 3))  18.9 us

profile of v1, /device:TPU:13, one launch (start us, length us, event | category | flops | bytes accessed | tf_op | source)
XLA Modules:
  0.0 178.9 jit_solution(16488090491097907571)
XLA Ops:
  0.7 0.7 broadcast_in_dim.24.live_ref
  1.3 0.7 convert_element_type.9
  2.0 1.4 select_reduce_fusion.coef_ref
  3.4 28.7 %copy.19 = bf16[1,2048,2,1408]{1,3,2,0:T(8,128)(2,1)} copy(bf16[1,2048,2,1408]{3,2,1,0:T(2,128)(2,1)} %param.18) | data formatting | bytes 23068672 | tf_op args[7]
  32.1 28.6 %copy.20 = bf16[11,2048,2,128]{3,2,1,0:T(2,128)(2,1)} copy(bf16[11,2048,2,128]{1,3,0,2:T(8,128)(2,1)} %bitcast.8) | data formatting | bytes 23068672 | tf_op jit(solution)/shard_map/transpose | solution.py:522
  60.7 0.0 copy-start
  60.7 18.9 %reshape.30.w_in_hbm = bf16[11,2048,256]{2,1,0:T(8,128)(2,1)} reshape(bf16[11,2048,2,128]{3,2,1,0:T(2,128)(2,1)} %copy.20) | data formatting | bytes 23068672 | tf_op jit(solution)/shard_map/reshape | solution.py:522
  79.6 0.0 copy-done
  79.6 0.7 tile.9.lens_ref
  80.3 97.0 %shard_map.109 = bf16[32,2048]{1,0:T(8,128)(2,1)} custom-call(bf16[3,32,2048]{2,1,0:T(8,128)(2,1)} %bitcast.10, s32[8,1,128]{2,1,0:T(1,128)} %tile.9.lens_ref, bf16[2,8,32,128,256]{4,3,2,1,0:T(8,128)(2,1)} %kv_hbm.1, bf16[256,2048]{1,0:T(8,128)(2,1)} %w_out_ref.1, bf16[32,2048]{1,0:T(8,128)(2,1)} %hidden_ref.1, f32[1,2048]{1,0:T(1,128)} %bitcast.11, ...), custom_call_target="tpu_custom_call" | custom-call | tf_op jit(solution)/shard_map/pallas_call | solution.py:529
  177.3 1.6 copy.23
  (2 shorter events, 0.0 us)
Async XLA Ops:
  60.7 18.9 %copy-start = (s32[8,32]{1,0:T(8,128)S(1)}, s32[8,32]{1,0:T(8,128)}, u32[]{:S(2)}) copy-start(s32[8,32]{1,0:T(8,128)} %param.14) | copy-start | bytes 3076

commit v2 on v1

--- a/solution.py
+++ b/solution.py
@@ -404,7 +404,7 @@
         s_copy(e, sister).wait_recv()
 
     expert = me * 2 + rep
-    tiles = w_in_buf.shape[0]
+    tiles = w_in_buf.shape[2] // LANES
     half = owners * block
     step = 2 * LANES
 
@@ -412,9 +412,11 @@
         @pl.loop(0, tiles)
         def _(n):
             rows = rows_all[side, :, :, :width].reshape(half, width)
-            both = jnp.dot(rows, w_in_buf[n], preferred_element_type=F32)
+            lanes = pl.ds(pl.multiple_of(n * LANES, LANES), LANES)
+            both_w = jnp.concatenate([w_in_buf[0, :, lanes], w_in_buf[1, :, lanes]], axis=1)
+            both = jnp.dot(rows, both_w, preferred_element_type=F32)
             gate, up = both[:, :LANES], both[:, LANES:]
-            hidden_buf[:, pl.ds(pl.multiple_of(n * LANES, LANES), LANES)] = (
+            hidden_buf[:, lanes] = (
                 gate / (1.0 + jnp.exp(-gate)) * up
             ).astype(BF16)
 
@@ -511,7 +513,6 @@
     positions = kv_cache.shape[3]
     cols = owners // 2
     inner = w_down.shape[1]
-    tiles = inner // LANES
     fresh = jnp.transpose(qkv_new, (1, 0, 2))
     lens = jnp.tile(cache_len, (1, LANES // block)).reshape(owners, 1, LANES)
     live = jnp.arange(block, dtype=jnp.int32) < row_counts[0]
@@ -519,9 +520,7 @@
     hits = (route_ids[:, :, None] == lane[None, None, :]) & live[:, None, None]
     coef = jnp.sum(jnp.where(hits, route_weight.astype(F32)[:, :, None], 0.0), axis=1).astype(BF16)
     live_wide = jnp.broadcast_to(live[:, None], (block, LANES)).astype(F32)
-    w_tiles = jnp.transpose(w_in.reshape(width, 2, tiles, LANES), (2, 0, 1, 3)).reshape(
-        tiles, width, 2 * LANES
-    )
+    w_planes = jnp.transpose(w_in.reshape(width, 2, inner), (1, 0, 2))
     vmem = pl.BlockSpec(memory_space=pltpu.VMEM)
     hbm = pl.BlockSpec(memory_space=pl.ANY)
     dma = pltpu.SemaphoreType.DMA
@@ -540,7 +539,7 @@
             pltpu.VMEM(wide, BF16),
             pltpu.VMEM((block, width), F32),
             pltpu.VMEM((2, owners, block, width + LANES), BF16),
-            pltpu.VMEM((tiles, width, 2 * LANES), BF16),
+            pltpu.VMEM((2, width, inner), BF16),
             pltpu.VMEM((inner, width), BF16),
             pltpu.VMEM((owners * block, inner), BF16),
             pltpu.VMEM((owners, block, width), BF16),
@@ -581,7 +580,7 @@
         moe_gain.reshape(1, width),
         coef,
         live_wide,
-        w_tiles,
+        w_planes,
         w_down.reshape(inner, width),
     )
 

time: 181 us -> 115 us (0.64); the launches traced: 179 us -> 115 us
  local copies, waits for them, and re-layouts: 79.1 us -> 14.9 us
    transpose x1 -> x0, local copies, waits for them, and re-layouts: 28.6 us -> none  [fast_local(): jnp.transpose(w_in.reshape(width, 2, tiles, LANES), (2, 0, 1, 3))]
    reshape x1 -> x0, local copies, waits for them, and re-layouts: 18.9 us -> none  [fast_local(): jnp.transpose(w_in.reshape(width, 2, tiles, LANES), (2, 0, 1, 3))]
    unnamed x4 -> x2, local copies, waits for them, and re-layouts: 30.2 us -> 12.8 us
where the time goes in v2:
time: 115 us
  Pallas kernels  97.2 us (85%)
  local copies, waits for them, and re-layouts  14.9 us (13%)
  other arithmetic  2.1 us (2%)
    pallas_call x1, Pallas kernels, fast_local(): pl.pallas_call(functools.partial(layer_kernel, owners), out_shape=jax.Sha...  97.2 us
    unnamed x2, local copies, waits for them, and re-layouts  12.8 us

profile of v2, /device:TPU:13, one launch (start us, length us, event | category | flops | bytes accessed | tf_op | source)
XLA Modules:
  0.0 114.9 jit_solution(13910753460197122275)
XLA Ops:
  0.7 0.7 convert_element_type.9
  1.4 1.4 %select_reduce_fusion.coef_ref = bf16[32,128]{1,0:T(8,128)(2,1)} fusion(f32[32,6]{0,1:T(8,128)S(1)} %convert_element_type.9, s32[32,6]{0,1:T(8,128)} %param.20, pred[32]{0:T(512)(128)(4,1)S(1)} %get-tuple-element.5), kind=kLoop, calls=%fused_computation.1 | loop fusion | flops 94208 | bytes 9760 | tf_op jit(solution)/shard_map/reduce_sum | solution.py:521
  2.8 0.7 broadcast_in_dim.24.live_ref
  3.4 0.7 tile.8
  4.1 0.7 tile.9.lens_ref
  4.8 11.3 %copy.17 = bf16[1,2048,2,1408]{3,1,2,0:T(8,128)(2,1)} copy(bf16[1,2048,2,1408]{3,2,1,0:T(2,128)(2,1)} %param.18) | data formatting | bytes 23068672 | tf_op args[7]
  16.1 97.2 %shard_map.109 = bf16[32,2048]{1,0:T(8,128)(2,1)} custom-call(bf16[3,32,2048]{2,1,0:T(8,128)(2,1)} %bitcast.12, s32[8,1,128]{2,1,0:T(1,128)} %tile.9.lens_ref, bf16[2,8,32,128,256]{4,3,2,1,0:T(8,128)(2,1)} %kv_hbm.1, bf16[256,2048]{1,0:T(8,128)(2,1)} %w_out_ref.1, bf16[32,2048]{1,0:T(8,128)(2,1)} %hidden_ref.1, f32[1,2048]{1,0:T(1,128)} %bitcast.13, ...), custom_call_target="tpu_custom_call" | custom-call | tf_op jit(solution)/shard_map/pallas_call | solution.py:528
  113.3 1.6 %copy.20 = bf16[32,2048]{1,0:T(8,128)(2,1)} copy(bf16[32,2048]{1,0:T(8,128)(2,1)} %shard_map.109) | data formatting | bytes 262144
  (1 shorter events, 0.0 us)

commit v3 on v2

--- a/solution.py
+++ b/solution.py
@@ -146,8 +146,9 @@
     w_out_ref,
     hidden_ref,
     gain_ref,
-    coef_ref,
-    live_ref,
+    ids_ref,
+    gate_ref,
+    count_ref,
     w_in_hbm,
     w_down_hbm,
     out_ref,
@@ -162,9 +163,8 @@
     w_in_buf,
     w_down_buf,
     hidden_buf,
-    y_out,
+    y_all,
     y_in,
-    y_own,
     pair_out2,
     pair_in2,
     col_out2,
@@ -247,6 +247,14 @@
 
     q_buf[me] = qkv_ref[:, :, pl.ds(pl.multiple_of(me * part, part), part)]
 
+    is_live = lax.broadcasted_iota(jnp.int32, (block, 1), 0) < count_ref[0]
+    lane_id = lax.broadcasted_iota(jnp.int32, (block, LANES), 1)
+    gates = gate_ref[...].astype(F32)
+    coef = jnp.zeros((block, LANES), F32)
+    for k in range(TOPK):
+        coef += jnp.where(lane_id == ids_ref[:, k : k + 1], gates[:, k : k + 1], 0.0)
+    rows_all[mx, rep, mz, :, width:] = jnp.where(is_live, coef, 0.0).astype(BF16)
+
     lane_row = lax.broadcasted_iota(jnp.int32, (positions, LANES), 1) % block
     pos_of = lax.broadcasted_iota(jnp.int32, (positions, LANES), 0)
     head_of = lax.broadcasted_iota(jnp.int32, (block, part), 1) // HEAD_DIM
@@ -281,7 +289,8 @@
             lax.broadcasted_iota(jnp.int32, (block, LANES), 1) % block
         )
         own = jnp.sum(jnp.where(diag, fresh, 0.0), axis=0, keepdims=True) * scale
-        in_cache = pos_of < lens_ref[owner]
+        lens = jnp.concatenate([lens_ref[pl.ds(owner, 1), :]] * (LANES // block), axis=1)
+        in_cache = pos_of < lens
         scores = jnp.where(in_cache, scores * scale, masked_score)
         top = jnp.maximum(jnp.max(scores, axis=0, keepdims=True), own)
         weights = jnp.where(in_cache, jnp.exp(scores - top), 0.0)
@@ -365,23 +374,49 @@
     wide = residual.astype(F32)
     total[...] = wide
     inverse = lax.rsqrt(jnp.mean(wide * wide, axis=1, keepdims=True) + epsilon)
-    rows_all[rep, me, :, :width] = (wide * inverse * gain_ref[...]).astype(BF16)
-    rows_all[rep, me, :, width:] = coef_ref[...]
+    rows_all[mx, rep, mz, :, :width] = (wide * inverse * gain_ref[...]).astype(BF16)
+
+    def row_copy(e, side, send, ep=None, core=None):
+        at = rows_all.at[e % 2, side, e // 2]
+        return remote(at, at, send, g_recv.at[e % 2, side, e // 2], ep=ep, core=core)
 
     def z_copy(z, e):
-        return remote(
-            rows_all.at[rep, e], rows_all.at[rep, e], z_send.at[z], g_recv.at[rep, e], ep=z * 2 + mx
-        )
+        return row_copy(e, rep, z_send.at[z], ep=z * 2 + mx)
 
     def x_copy(e):
-        return remote(
-            rows_all.at[rep, e], rows_all.at[rep, e], x_send.at[e], g_recv.at[rep, e], ep=across
-        )
+        return row_copy(e, rep, x_send.at[e], ep=across)
 
     def s_copy(e, side):
-        return remote(
-            rows_all.at[side, e], rows_all.at[side, e], s_send.at[e], g_recv.at[side, e], core=sister
-        )
+        return row_copy(e, side, s_send.at[e], core=sister)
+
+    def y_copy(x):
+        return remote(y_all.at[x, sister], y_in.at[x], y_send.at[x], y_recv.at[x], core=sister)
+
+    expert = me * 2 + rep
+    tiles = w_in_buf.shape[2] // LANES
+    half = owners * block
+    step = 2 * LANES
+
+    def experts(x):
+        @pl.loop(0, tiles)
+        def _(n):
+            rows = rows_all[x, :, :, :, :width].reshape(half, width)
+            lanes = pl.ds(pl.multiple_of(n * LANES, LANES), LANES)
+            both_w = jnp.concatenate([w_in_buf[0, :, lanes], w_in_buf[1, :, lanes]], axis=1)
+            both = jnp.dot(rows, both_w, preferred_element_type=F32)
+            gate, up = both[:, :LANES], both[:, LANES:]
+            hidden_buf[:, lanes] = (gate / (1.0 + jnp.exp(-gate)) * up).astype(BF16)
+
+        coefs = rows_all[x, :, :, :, width:].reshape(half, LANES).astype(F32)
+        lane = lax.broadcasted_iota(jnp.int32, (half, LANES), 1)
+        factor = jnp.sum(jnp.where(lane == expert, coefs, 0.0), axis=1, keepdims=True)
+
+        @pl.loop(0, width // step)
+        def _(n):
+            lanes = pl.ds(pl.multiple_of(n * step, step), step)
+            made = jnp.dot(hidden_buf[...], w_down_buf[:, lanes], preferred_element_type=F32)
+            made = made.astype(BF16).astype(F32) * factor
+            y_all[x, :, :, :, lanes] = made.astype(BF16).reshape(2, cols, block, step)
 
     for j in range(1, cols):
         z_copy((mz + j) % cols, me).start()
@@ -392,55 +427,21 @@
         z_copy(e // 2, e).wait_recv()
         x_copy(e).start()
         s_copy(e, rep).start()
+    in_copy.wait()
+    down_copy.wait()
+    for z in range(cols):
+        s_copy(z * 2 + mx, sister).wait_recv()
+    experts(mx)
+    y_copy(mx).start()
     for j in range(cols):
         e = ((mz + j) % cols) * 2 + 1 - mx
         x_copy(e).wait_recv()
         s_copy(e, rep).start()
-    in_copy.wait()
-    down_copy.wait()
-
-    @pl.loop(0, owners)
-    def _(e):
-        s_copy(e, sister).wait_recv()
-
-    expert = me * 2 + rep
-    tiles = w_in_buf.shape[2] // LANES
-    half = owners * block
-    step = 2 * LANES
-
-    def experts(side, store):
-        @pl.loop(0, tiles)
-        def _(n):
-            rows = rows_all[side, :, :, :width].reshape(half, width)
-            lanes = pl.ds(pl.multiple_of(n * LANES, LANES), LANES)
-            both_w = jnp.concatenate([w_in_buf[0, :, lanes], w_in_buf[1, :, lanes]], axis=1)
-            both = jnp.dot(rows, both_w, preferred_element_type=F32)
-            gate, up = both[:, :LANES], both[:, LANES:]
-            hidden_buf[:, lanes] = (
-                gate / (1.0 + jnp.exp(-gate)) * up
-            ).astype(BF16)
-
-        coefs = rows_all[side, :, :, width:].reshape(half, LANES).astype(F32)
-        lane = lax.broadcasted_iota(jnp.int32, (half, LANES), 1)
-        factor = jnp.sum(jnp.where(lane == expert, coefs, 0.0), axis=1, keepdims=True)
-
-        @pl.loop(0, width // step)
-        def _(n):
-            lanes = pl.ds(pl.multiple_of(n * step, step), step)
-            made = jnp.dot(hidden_buf[...], w_down_buf[:, lanes], preferred_element_type=F32)
-            store(lanes, (made.astype(BF16).astype(F32) * factor).reshape(owners, block, step))
-
-    def store_out(lanes, v):
-        y_out[:, :, lanes] = v.astype(BF16)
-
-    def store_own(lanes, v):
-        y_own[:, :, lanes] = v
-
-    experts(sister, store_out)
-    y_copy = remote(y_out, y_in, y_send, y_recv, core=sister)
-    y_copy.start()
-    experts(rep, store_own)
-    y_copy.wait()
+    for z in range(cols):
+        s_copy(z * 2 + 1 - mx, sister).wait_recv()
+    experts(1 - mx)
+    y_copy(1 - mx).start()
+    y_copy(1 - mx).wait_recv()
 
     def pair_copy2(z):
         return remote(
@@ -454,14 +455,15 @@
 
     for j in range(cols):
         z = (mz + 1 + j) % cols
-        e = z * 2 + 1 - mx
-        pair_out2[z] = (y_own[e] + y_in[e].astype(F32)).astype(BF16)
+        made = y_all[1 - mx, rep, z].astype(F32) + y_in[1 - mx, z].astype(F32)
+        pair_out2[z] = made.astype(BF16)
         pair_copy2(z).start()
+    y_copy(mx).wait_recv()
     for j in range(cols):
         z = (mz + 1 + j) % cols
-        e = z * 2 + mx
+        made = y_all[mx, rep, z].astype(F32) + y_in[mx, z].astype(F32)
         pair_copy2(z).wait_recv()
-        mine = y_own[e] + y_in[e].astype(F32) + pair_in2[z].astype(F32)
+        mine = made + pair_in2[z].astype(F32)
         if j < cols - 1:
             col_out2[z] = mine.astype(BF16)
             col_copy2(z, mz).start()
@@ -471,13 +473,15 @@
         z = (mz + j) % cols
         col_copy2(z, z).wait_recv()
         total[...] += col_in2[z].astype(F32)
-    out_ref[...] = jnp.where(live_ref[:, :1] > 0.0, total[...], 0.0).astype(BF16)
+    out_ref[...] = jnp.where(is_live, total[...], 0.0).astype(BF16)
 
     @pl.loop(1, owners)
     def _(i):
         to = (me + i) % owners
         remote(q_part(to), q_buf.at[me], q_send.at[to], q_recv.at[me], ep=to).wait_send()
 
+    for x in range(2):
+        y_copy(x).wait_send()
     for z in range(cols):
         pair_copy(z).wait_send()
         pair_copy2(z).wait_send()
@@ -514,21 +518,16 @@
     cols = owners // 2
     inner = w_down.shape[1]
     fresh = jnp.transpose(qkv_new, (1, 0, 2))
-    lens = jnp.tile(cache_len, (1, LANES // block)).reshape(owners, 1, LANES)
-    live = jnp.arange(block, dtype=jnp.int32) < row_counts[0]
-    lane = jnp.arange(LANES, dtype=jnp.int32)
-    hits = (route_ids[:, :, None] == lane[None, None, :]) & live[:, None, None]
-    coef = jnp.sum(jnp.where(hits, route_weight.astype(F32)[:, :, None], 0.0), axis=1).astype(BF16)
-    live_wide = jnp.broadcast_to(live[:, None], (block, LANES)).astype(F32)
     w_planes = jnp.transpose(w_in.reshape(width, 2, inner), (1, 0, 2))
     vmem = pl.BlockSpec(memory_space=pltpu.VMEM)
     hbm = pl.BlockSpec(memory_space=pl.ANY)
+    smem = pl.BlockSpec(memory_space=pltpu.SMEM)
     dma = pltpu.SemaphoreType.DMA
     wide = (cols, block, width)
     return pl.pallas_call(
         functools.partial(layer_kernel, owners),
         out_shape=jax.ShapeDtypeStruct((block, width), BF16),
-        in_specs=[vmem, vmem, hbm, vmem, vmem, vmem, vmem, vmem, hbm, hbm],
+        in_specs=[vmem, vmem, hbm, vmem, vmem, vmem, vmem, vmem, smem, hbm, hbm],
         out_specs=vmem,
         scratch_shapes=[
             pltpu.VMEM((2, 2, block, positions, part), BF16),
@@ -538,13 +537,12 @@
             pltpu.VMEM(wide, BF16),
             pltpu.VMEM(wide, BF16),
             pltpu.VMEM((block, width), F32),
-            pltpu.VMEM((2, owners, block, width + LANES), BF16),
+            pltpu.VMEM((2, 2, cols, block, width + LANES), BF16),
             pltpu.VMEM((2, width, inner), BF16),
             pltpu.VMEM((inner, width), BF16),
             pltpu.VMEM((owners * block, inner), BF16),
-            pltpu.VMEM((owners, block, width), BF16),
-            pltpu.VMEM((owners, block, width), BF16),
-            pltpu.VMEM((owners, block, width), F32),
+            pltpu.VMEM((2, 2, cols, block, width), BF16),
+            pltpu.VMEM((2, cols, block, width), BF16),
             pltpu.VMEM(wide, BF16),
             pltpu.VMEM(wide, BF16),
             pltpu.VMEM(wide, BF16),
@@ -560,9 +558,9 @@
             dma((cols,)),
             dma((owners,)),
             dma((owners,)),
-            dma((2, owners)),
-            dma(()),
-            dma(()),
+            dma((2, 2, cols)),
+            dma((2,)),
+            dma((2,)),
             dma((cols,)),
             dma((cols,)),
             dma((cols,)),
@@ -573,13 +571,14 @@
         ),
     )(
         fresh,
-        lens,
+        cache_len,
         kv_cache,
         w_out,
         hidden_in,
         moe_gain.reshape(1, width),
-        coef,
-        live_wide,
+        route_ids,
+        route_weight,
+        row_counts,
         w_planes,
         w_down.reshape(inner, width),
     )

time: 115 us -> 112 us (0.974)
  other arithmetic: 2.1 us -> 0 us
  Pallas kernels: 97.2 us -> 95.2 us
    unnamed x2 -> x4, local copies, waits for them, and re-layouts: 12.8 us -> 15.6 us
    pallas_call x1, Pallas kernels: 97.2 us -> 95.2 us  [fast_local(): pl.pallas_call(functools.partial(layer_kernel, owners), out_shape=jax.Sha...]
    reduce_sum x1 -> x0, other arithmetic: 1.41 us -> none  [fast_local(): jnp.sum(jnp.where(hits, route_weight.astype(F32)[:, :, None], 0.0), axis=1)]
    another operation x2 -> x0, local copies, waits for them, and re-layouts: 1.37 us -> none  [fast_local(): lens = jnp.tile(cache_len, (1, LANES // block)).reshape(owners, 1, LANES)]
where the time goes in v3:
time: 112 us; the launch traced here: 111 us
  Pallas kernels  95.2 us (85%)
  local copies, waits for them, and re-layouts  15.6 us (14%)
    pallas_call x1, Pallas kernels, fast_local(): pl.pallas_call(functools.partial(layer_kernel, owners), out_shape=jax.Sha...  95.2 us
    unnamed x4, local copies, waits for them, and re-layouts  15.6 us

profile of v3, /device:TPU:13, one launch (start us, length us, event | category | flops | bytes accessed | tf_op | source)
XLA Modules:
  0.0 111.5 jit_solution(10569657438190032553)
XLA Ops:
  0.7 1.4 %copy.14.gate_ref = bf16[32,6]{1,0:T(8,128)(2,1)} copy(bf16[32,6]{0,1:T(8,128)(2,1)} %param.21) | data formatting | bytes 768 | tf_op args[10]
  2.0 1.4 %copy.13.ids_ref = s32[32,6]{1,0:T(8,128)} copy(s32[32,6]{0,1:T(8,128)} %param.20) | data formatting | bytes 1536 | tf_op args[9]
  3.4 11.3 %copy.16 = bf16[1,2048,2,1408]{3,1,2,0:T(8,128)(2,1)} copy(bf16[1,2048,2,1408]{3,2,1,0:T(2,128)(2,1)} %param.18) | data formatting | bytes 23068672 | tf_op args[7]
  14.6 95.2 %shard_map.109 = bf16[32,2048]{1,0:T(8,128)(2,1)} custom-call(bf16[3,32,2048]{2,1,0:T(8,128)(2,1)} %bitcast.10, s32[8,32]{1,0:T(8,128)} %lens_ref.1, bf16[2,8,32,128,256]{4,3,2,1,0:T(8,128)(2,1)} %kv_hbm.1, bf16[256,2048]{1,0:T(8,128)(2,1)} %w_out_ref.1, bf16[32,2048]{1,0:T(8,128)(2,1)} %hidden_ref.1, f32[1,2048]{1,0:T(1,128)} %bitcast.11, ...), custom_call_target="tpu_custom_call" | custom-call | tf_op jit(solution)/shard_map/pallas_call | solution.py:527
  109.9 1.6 %copy.19 = bf16[32,2048]{1,0:T(8,128)(2,1)} copy(bf16[32,2048]{1,0:T(8,128)(2,1)} %shard_map.109) | data formatting | bytes 262144

commit v4 on v3

--- a/solution.py
+++ b/solution.py
@@ -248,14 +248,17 @@
     q_buf[me] = qkv_ref[:, :, pl.ds(pl.multiple_of(me * part, part), part)]
 
     is_live = lax.broadcasted_iota(jnp.int32, (block, 1), 0) < count_ref[0]
-    lane_id = lax.broadcasted_iota(jnp.int32, (block, LANES), 1)
+    expert_id = lax.broadcasted_iota(jnp.int32, (LANES, LANES), 0)
     gates = gate_ref[...].astype(F32)
-    coef = jnp.zeros((block, LANES), F32)
+    ids = jnp.concatenate([ids_ref[...]] * (LANES // block), axis=1)
+    gates = jnp.concatenate([gates] * (LANES // block), axis=1)
+    coef = jnp.zeros((LANES, LANES), F32)
     for k in range(TOPK):
-        coef += jnp.where(lane_id == ids_ref[:, k : k + 1], gates[:, k : k + 1], 0.0)
+        coef += jnp.where(expert_id == ids[k : k + 1], gates[k : k + 1], 0.0)
+    coef = coef.T[:block]
     rows_all[mx, rep, mz, :, width:] = jnp.where(is_live, coef, 0.0).astype(BF16)
 
-    lane_row = lax.broadcasted_iota(jnp.int32, (positions, LANES), 1) % block
+    lane_row = lax.broadcasted_iota(jnp.int32, (1, LANES), 1) % block
     pos_of = lax.broadcasted_iota(jnp.int32, (positions, LANES), 0)
     head_of = lax.broadcasted_iota(jnp.int32, (block, part), 1) // HEAD_DIM
     row_mod = lax.broadcasted_iota(jnp.int32, (used, positions), 0) % block
@@ -576,8 +579,8 @@
         w_out,
         hidden_in,
         moe_gain.reshape(1, width),
-        route_ids,
-        route_weight,
+        route_ids.T,
+        route_weight.T,
         row_counts,
         w_planes,
         w_down.reshape(inner, width),

time: 112 us -> 109 us (0.973)
  local copies, waits for them, and re-layouts: 15.6 us -> 12.8 us
    unnamed x4 -> x2, local copies, waits for them, and re-layouts: 15.6 us -> 12.8 us
where the time goes in v4:
time: 109 us
  Pallas kernels  95.3 us (87%)
  local copies, waits for them, and re-layouts  12.8 us (12%)
    pallas_call x1, Pallas kernels, fast_local(): pl.pallas_call(functools.partial(layer_kernel, owners), out_shape=jax.Sha...  95.3 us
    unnamed x2, local copies, waits for them, and re-layouts  12.8 us

profile of v4, /device:TPU:13, one launch (start us, length us, event | category | flops | bytes accessed | tf_op | source)
XLA Modules:
  0.0 108.8 jit_solution(2749103540541598640)
XLA Ops:
  0.7 11.3 %copy.14 = bf16[1,2048,2,1408]{3,1,2,0:T(8,128)(2,1)} copy(bf16[1,2048,2,1408]{3,2,1,0:T(2,128)(2,1)} %param.18) | data formatting | bytes 23068672 | tf_op args[7]
  11.9 95.3 %shard_map.109 = bf16[32,2048]{1,0:T(8,128)(2,1)} custom-call(bf16[3,32,2048]{2,1,0:T(8,128)(2,1)} %bitcast.12, s32[8,32]{1,0:T(8,128)} %lens_ref.1, bf16[2,8,32,128,256]{4,3,2,1,0:T(8,128)(2,1)} %kv_hbm.1, bf16[256,2048]{1,0:T(8,128)(2,1)} %w_out_ref.1, bf16[32,2048]{1,0:T(8,128)(2,1)} %hidden_ref.1, f32[1,2048]{1,0:T(1,128)} %bitcast.13, ...), custom_call_target="tpu_custom_call" | custom-call | tf_op jit(solution)/shard_map/pallas_call | solution.py:530
  107.2 1.6 %copy.17 = bf16[32,2048]{1,0:T(8,128)(2,1)} copy(bf16[32,2048]{1,0:T(8,128)(2,1)} %shard_map.109) | data formatting | bytes 262144
